TPU v7x, 32 devices: a whole 2x2x4 slice. The times are simulated.
32 devices in a mesh: wide: 8 (over z, y), narrow: 4 (over x, core).
Axes of the slice: x: 2, y: 2, z: 4, core: 2. Of those that a mesh axis runs over, the one named last changes fastest.
Arguments:
- solution: float32 [8, 16384], P(None, ('wide', 'narrow')), may hold values from -6 to 6
- residual: float32 [8, 16384], P(None, ('wide', 'narrow')), may hold values from -600 to 600
- direction: float32 [8, 16384], P(None, ('wide', 'narrow')), may hold values from -600 to 600
- error_var: float32 [16384], P(('wide', 'narrow')), may hold values from 0.25 to 2
- footprint: bfloat16 [16384, 4, 128], P(('wide', 'narrow')), may hold values from -0.25 to 0.25
- tiles: int32 [16384, 4], P(('wide', 'narrow')), may hold values from 0 to 1279
- window: int32 [16384, 1], P(('wide', 'narrow')), may hold values from 0 to 7; in each aligned block of 512 rows (0 to 511, 512 to 1023, ...) at most 160 rows name the same one
- temporal: bfloat16 [320, 320], replicated, may hold values from -40 to 40, as said below
- spatial_lat: bfloat16 [128, 128], replicated, may hold values from -40 to 40, as said below
- spatial_lon: bfloat16 [128, 128], replicated, may hold values from -40 to 40, as said below
Outputs:
- solution_new: float32 [8, 16384], P(None, ('wide', 'narrow'))
- residual_new: float32 [8, 16384], P(None, ('wide', 'narrow'))
- direction_new: float32 [8, 16384], P(None, ('wide', 'narrow'))
Inputs may be any that keep to these rules, and one draw needn't show every extreme that they name: At most 160 of the observations held by one device share a window, and some device reaches that in every draw. `temporal`: A symmetric positive definite covariance. `spatial_lat`: A symmetric positive definite covariance. `spatial_lon`: A symmetric positive definite covariance.
All inputs are finite; a program needn't handle non-finite values.
Results may differ from a plain program's by a relative error of at most 0.004.
Values may be sent and summed in bfloat16 or wider, within the bound.
A program may use at most 128 MiB of HBM per device.

v0:
```python
import math
import jax
import jax.numpy as jnp
from jax import lax
from jax.sharding import PartitionSpec as P

HIGHEST = lax.Precision.HIGHEST


def chol_solve(matrix, right):
    chol_low = jnp.linalg.cholesky(matrix)
    half_solve = lax.linalg.triangular_solve(chol_low, right, left_side=True, lower=True)
    return lax.linalg.triangular_solve(
        chol_low, half_solve, left_side=True, lower=True, transpose_a=True
    )


def gram_matrix(left, right):
    return jnp.dot(left, right.T, precision=HIGHEST)


def on_device(
    solution,
    residual,
    direction,
    error_var,
    footprint,
    tiles,
    window,
    temporal,
    spatial_lat,
    spatial_lon,
):
    n_wide = lax.axis_size("wide")
    n_narrow = lax.axis_size("narrow")
    rhs_count, obs_dev = direction.shape
    days_total = temporal.shape[0]
    day_dev = days_total // n_wide
    lat_total = spatial_lat.shape[0]
    lat_band = lat_total // n_narrow
    lon_count = spatial_lon.shape[0]
    tile_count = tiles.shape[1]
    capacity = obs_dev * 5 // (2 * n_wide)
    slot_total = n_wide * capacity
    tiles_local = day_dev * lat_band
    window_id = window[:, 0]
    dir_half = direction.astype(jnp.bfloat16)
    matches = (window_id[:, None] == jnp.arange(n_wide, dtype=jnp.int32)[None, :]).astype(jnp.int32)
    before = jnp.cumsum(matches, axis=0) - matches
    position = jnp.sum(before * matches, axis=1)
    slot_index = window_id * capacity + position
    source = (
        jnp.full((slot_total,), obs_dev, jnp.int32)
        .at[slot_index]
        .set(jnp.arange(obs_dev, dtype=jnp.int32))
    )
    foot_rows = jnp.concatenate(
        [
            footprint.reshape(obs_dev, tile_count * lon_count),
            jnp.zeros((1, tile_count * lon_count), jnp.bfloat16),
        ],
        0,
    )
    dir_rows = jnp.concatenate([dir_half.T, jnp.zeros((1, rhs_count), jnp.bfloat16)], 0)
    tile_rows = jnp.concatenate([tiles, jnp.zeros((1, tile_count), jnp.int32)], 0)
    recv_foot, recv_dir, recv_tiles = (
        lax.all_to_all(
            foot_rows[source].reshape(n_wide, capacity, tile_count * lon_count),
            "wide",
            split_axis=0,
            concat_axis=0,
            tiled=True,
        ),
        lax.all_to_all(
            dir_rows[source].reshape(n_wide, capacity, rhs_count),
            "wide",
            split_axis=0,
            concat_axis=0,
            tiled=True,
        ),
        lax.all_to_all(
            tile_rows[source].reshape(n_wide, capacity, tile_count),
            "wide",
            split_axis=0,
            concat_axis=0,
            tiled=True,
        ),
    )
    block_size = math.gcd(slot_total, 128)
    block_count = slot_total // block_size
    rows_block = block_size * tile_count
    foot_blocks = recv_foot.reshape(block_count, rows_block, lon_count)
    dir_blocks = jnp.repeat(recv_dir.reshape(slot_total, rhs_count), tile_count, axis=0).reshape(
        block_count, rows_block, rhs_count
    )
    id_blocks = recv_tiles.reshape(block_count, rows_block)
    tile_range = jnp.arange(tiles_local, dtype=jnp.int32)

    def adjoint_step(accum, inputs):
        foot_block, dir_block, id_block = inputs
        onehot = (id_block[None, :] == tile_range[:, None]).astype(jnp.bfloat16)
        weighted = (onehot[:, None, :] * dir_block.T[None, :, :]).reshape(
            tiles_local * rhs_count, rows_block
        )
        return (accum + jnp.dot(weighted, foot_block, preferred_element_type=jnp.float32), None)

    start_accum = jnp.zeros((tiles_local * rhs_count, lon_count), jnp.float32)
    accum, _ = lax.scan(adjoint_step, start_accum, (foot_blocks, dir_blocks, id_blocks))
    flat_flux = accum.astype(jnp.bfloat16).reshape(day_dev, lat_band * rhs_count * lon_count)
    all_days = lax.all_to_all(flat_flux, "wide", split_axis=1, concat_axis=0, tiled=True)
    mixed_days = jnp.dot(temporal, all_days, preferred_element_type=jnp.float32).astype(
        jnp.bfloat16
    )
    timed_flux = lax.all_to_all(mixed_days, "wide", split_axis=0, concat_axis=1, tiled=True)
    timed_flux = timed_flux.reshape(day_dev, lat_band, rhs_count, lon_count)
    narrow_index = lax.axis_index("narrow")
    lat_rows = lax.dynamic_slice_in_dim(spatial_lat, narrow_index * lat_band, lat_band, 0)
    lat_sum = jnp.einsum(
        "ab,dbrl->darl",
        lat_rows,
        lax.all_gather(timed_flux, "narrow", axis=1, tiled=True),
        preferred_element_type=jnp.float32,
    )
    spread_lat = lat_sum.astype(jnp.bfloat16)
    smoothed = jnp.dot(
        spread_lat.reshape(-1, lon_count), spatial_lon.T, preferred_element_type=jnp.float32
    ).astype(jnp.bfloat16)
    flux_table = smoothed.reshape(tiles_local, rhs_count * lon_count)

    def forward_step(accum_dummy, inputs):
        foot_block, id_block = inputs
        picked = flux_table[id_block].reshape(rows_block, rhs_count, lon_count)
        return (
            accum_dummy,
            jnp.einsum("jrl,jl->jr", picked, foot_block, preferred_element_type=jnp.float32),
        )

    _, model_rows = lax.scan(forward_step, jnp.zeros((), jnp.float32), (foot_blocks, id_blocks))
    back_rows = (
        model_rows.reshape(slot_total, tile_count, rhs_count)
        .sum(axis=1)
        .reshape(n_wide, capacity, rhs_count)
    )
    home_rows = lax.all_to_all(back_rows, "wide", split_axis=0, concat_axis=0, tiled=True).reshape(
        slot_total, rhs_count
    )
    model_part = home_rows[slot_index].T
    model_image = model_part + error_var[None, :] * direction
    curvature, res_norm = lax.psum(
        (gram_matrix(direction, model_image), gram_matrix(residual, residual)), ("wide", "narrow")
    )
    sym = 0.5 * (curvature + curvature.T)
    step_matrix = chol_solve(sym, res_norm)
    residual_new = residual - jnp.dot(step_matrix.T, model_image, precision=HIGHEST)
    norm_new = lax.psum(gram_matrix(residual_new, residual_new), ("wide", "narrow"))
    solution_new = solution + jnp.dot(step_matrix.T, direction, precision=HIGHEST)
    ratio_matrix = chol_solve(res_norm, norm_new)
    direction_new = residual_new + jnp.dot(ratio_matrix.T, direction, precision=HIGHEST)
    return (solution_new, residual_new, direction_new)


def solution(mesh):
    in_specs = (
        P(None, ("wide", "narrow")),
        P(None, ("wide", "narrow")),
        P(None, ("wide", "narrow")),
        P(("wide", "narrow")),
        P(("wide", "narrow"), None, None),
        P(("wide", "narrow"), None),
        P(("wide", "narrow"), None),
        P(),
        P(),
        P(),
    )
    out_specs = (
        P(None, ("wide", "narrow")),
        P(None, ("wide", "narrow")),
        P(None, ("wide", "narrow")),
    )
    return jax.shard_map(
        on_device, mesh=mesh, in_specs=in_specs, out_specs=out_specs, check_vma=False
    )
```

profile of v0, /device:TPU:0, one launch (start us, length us, event | category | flops | bytes accessed | tf_op | source)
XLA Modules:
  0.0 548.3 jit_solution(6296830245109133020)
XLA Ops:
  18.0 7.3 %all-to-all-start = ((s32[8,160,4]{1,2,0:T(4,128)}), s32[8,160,4]{1,2,0:T(4,128)S(1)}, u32[]{:S(2)}, u32[]{:S(2)}) async-start(s32[8,160,4]{1,2,0:T(4,128)} %copy.140), calls=%async_computation | async-start | bytes 65536 | tf_op jit(solution)/shard_map/all_to_all | solution.py:81
  35.5 4.7 gather_fusion.3
  47.8 28.6 %all-to-all-done.2 = bf16[8,160,512]{2,1,0:T(8,128)(2,1)S(1)} async-done(((bf16[8,160,512]{2,1,0:T(8,128)(2,1)}), bf16[8,160,512]{2,1,0:T(8,128)(2,1)S(1)}, u32[]{:S(2)}, u32[]{:S(2)}) %all-to-all-start.2) | async-done | bytes 1310752 | tf_op jit(solution)/shard_map/all_to_all | solution.py:67
  77.3 68.1 %while.22 = (s32[]{:T(128)}, f32[10240,128]{1,0:T(8,128)}, s32[10,512]{1,0:T(8,128)S(1)}, bf16[10,512,8]{1,2,0:T(8,128)(2,1)S(1)}, bf16[10,512,128]{2,1,0:T(8,128)(2,1)S(1)}, /*index=5*/s32[]{:T(128)}, s32[]{:T(128)}) while((s32[]{:T(128)}, f32[10240,128]{1,0:T(8,128)}, s32[10,512]{1,0:T(8,128)S(1)}, ...), condition=%wide.region_5.6_spmd.clone, body=%wide.region_4.5_spmd.clone.sunk | while | flops 1351352320 | bytes 13269091 | solution.py:108
  77.9 4.7 convolution_add_fusion.4
  83.2 6.4 %convolution_add_fusion.4 = f32[10240,128]{1,0:T(8,128)} fusion(f32[10240,128]{1,0:T(8,128)} %get-tuple-element.209, bf16[8,512]{1,0:T(8,128)(2,1)S(1)} %dynamic-slice_bitcast_fusion.5, bf16[1280,512]{1,0:T(8,128)(2,1)S(1)} %fusion.68, pred[]{:T(512)S(6)} %compare.30, bf16[10,512,128]{2,1,0:T(8,128)(2,1)S(1)} %get-tuple-element.219, ...), kind=kOutput, calls=%fused_computation.13.clone.1 | convolution fusion | flops 1350041600 | bytes 11935749 | tf_op jit(solution)/shard_map/while/body/eval_jaxpr/dot_general | solution.py:105
  90.2 6.4 %convolution_add_fusion.4 = f32[10240,128]{1,0:T(8,128)} fusion(f32[10240,128]{1,0:T(8,128)} %get-tuple-element.209, bf16[8,512]{1,0:T(8,128)(2,1)S(1)} %dynamic-slice_bitcast_fusion.5, bf16[1280,512]{1,0:T(8,128)(2,1)S(1)} %fusion.68, pred[]{:T(512)S(6)} %compare.30, bf16[10,512,128]{2,1,0:T(8,128)(2,1)S(1)} %get-tuple-element.219, ...), kind=kOutput, calls=%fused_computation.13.clone.1 | convolution fusion | flops 1350041600 | bytes 11935749 | tf_op jit(solution)/shard_map/while/body/eval_jaxpr/dot_general | solution.py:105
  97.2 6.4 %convolution_add_fusion.4 = f32[10240,128]{1,0:T(8,128)} fusion(f32[10240,128]{1,0:T(8,128)} %get-tuple-element.209, bf16[8,512]{1,0:T(8,128)(2,1)S(1)} %dynamic-slice_bitcast_fusion.5, bf16[1280,512]{1,0:T(8,128)(2,1)S(1)} %fusion.68, pred[]{:T(512)S(6)} %compare.30, bf16[10,512,128]{2,1,0:T(8,128)(2,1)S(1)} %get-tuple-element.219, ...), kind=kOutput, calls=%fused_computation.13.clone.1 | convolution fusion | flops 1350041600 | bytes 11935749 | tf_op jit(solution)/shard_map/while/body/eval_jaxpr/dot_general | solution.py:105
  104.1 6.4 %convolution_add_fusion.4 = f32[10240,128]{1,0:T(8,128)} fusion(f32[10240,128]{1,0:T(8,128)} %get-tuple-element.209, bf16[8,512]{1,0:T(8,128)(2,1)S(1)} %dynamic-slice_bitcast_fusion.5, bf16[1280,512]{1,0:T(8,128)(2,1)S(1)} %fusion.68, pred[]{:T(512)S(6)} %compare.30, bf16[10,512,128]{2,1,0:T(8,128)(2,1)S(1)} %get-tuple-element.219, ...), kind=kOutput, calls=%fused_computation.13.clone.1 | convolution fusion | flops 1350041600 | bytes 11935749 | tf_op jit(solution)/shard_map/while/body/eval_jaxpr/dot_general | solution.py:105
  111.1 6.4 %convolution_add_fusion.4 = f32[10240,128]{1,0:T(8,128)} fusion(f32[10240,128]{1,0:T(8,128)} %get-tuple-element.209, bf16[8,512]{1,0:T(8,128)(2,1)S(1)} %dynamic-slice_bitcast_fusion.5, bf16[1280,512]{1,0:T(8,128)(2,1)S(1)} %fusion.68, pred[]{:T(512)S(6)} %compare.30, bf16[10,512,128]{2,1,0:T(8,128)(2,1)S(1)} %get-tuple-element.219, ...), kind=kOutput, calls=%fused_computation.13.clone.1 | convolution fusion | flops 1350041600 | bytes 11935749 | tf_op jit(solution)/shard_map/while/body/eval_jaxpr/dot_general | solution.py:105
  118.1 6.4 %convolution_add_fusion.4 = f32[10240,128]{1,0:T(8,128)} fusion(f32[10240,128]{1,0:T(8,128)} %get-tuple-element.209, bf16[8,512]{1,0:T(8,128)(2,1)S(1)} %dynamic-slice_bitcast_fusion.5, bf16[1280,512]{1,0:T(8,128)(2,1)S(1)} %fusion.68, pred[]{:T(512)S(6)} %compare.30, bf16[10,512,128]{2,1,0:T(8,128)(2,1)S(1)} %get-tuple-element.219, ...), kind=kOutput, calls=%fused_computation.13.clone.1 | convolution fusion | flops 1350041600 | bytes 11935749 | tf_op jit(solution)/shard_map/while/body/eval_jaxpr/dot_general | solution.py:105
  125.1 6.4 %convolution_add_fusion.4 = f32[10240,128]{1,0:T(8,128)} fusion(f32[10240,128]{1,0:T(8,128)} %get-tuple-element.209, bf16[8,512]{1,0:T(8,128)(2,1)S(1)} %dynamic-slice_bitcast_fusion.5, bf16[1280,512]{1,0:T(8,128)(2,1)S(1)} %fusion.68, pred[]{:T(512)S(6)} %compare.30, bf16[10,512,128]{2,1,0:T(8,128)(2,1)S(1)} %get-tuple-element.219, ...), kind=kOutput, calls=%fused_computation.13.clone.1 | convolution fusion | flops 1350041600 | bytes 11935749 | tf_op jit(solution)/shard_map/while/body/eval_jaxpr/dot_general | solution.py:105
  132.1 6.4 %convolution_add_fusion.4 = f32[10240,128]{1,0:T(8,128)} fusion(f32[10240,128]{1,0:T(8,128)} %get-tuple-element.209, bf16[8,512]{1,0:T(8,128)(2,1)S(1)} %dynamic-slice_bitcast_fusion.5, bf16[1280,512]{1,0:T(8,128)(2,1)S(1)} %fusion.68, pred[]{:T(512)S(6)} %compare.30, bf16[10,512,128]{2,1,0:T(8,128)(2,1)S(1)} %get-tuple-element.219, ...), kind=kOutput, calls=%fused_computation.13.clone.1 | convolution fusion | flops 1350041600 | bytes 11935749 | tf_op jit(solution)/shard_map/while/body/eval_jaxpr/dot_general | solution.py:105
  139.0 6.4 %convolution_add_fusion.4 = f32[10240,128]{1,0:T(8,128)} fusion(f32[10240,128]{1,0:T(8,128)} %get-tuple-element.209, bf16[8,512]{1,0:T(8,128)(2,1)S(1)} %dynamic-slice_bitcast_fusion.5, bf16[1280,512]{1,0:T(8,128)(2,1)S(1)} %fusion.68, pred[]{:T(512)S(6)} %compare.30, bf16[10,512,128]{2,1,0:T(8,128)(2,1)S(1)} %get-tuple-element.219, ...), kind=kOutput, calls=%fused_computation.13.clone.1 | convolution fusion | flops 1350041600 | bytes 11935749 | tf_op jit(solution)/shard_map/while/body/eval_jaxpr/dot_general | solution.py:105
  155.5 62.8 %all_to_all.55 = bf16[40,8,4096]{2,0,1:T(8,128)(2,1)S(1)} all-to-all(bf16[40,8,4096]{2,0,1:T(8,128)(2,1)S(1)} %copy.147), channel_id=1, replica_groups=mesh['wide'=8,'narrow'=4] {'wide'}, dimensions={1} | all-to-all | bytes 5242880 | tf_op jit(solution)/shard_map/all_to_all | solution.py:110
  219.8 62.7 %all_to_all.56 = bf16[8,40,4096]{2,1,0:T(8,128)(2,1)S(1)} all-to-all(bf16[8,40,4096]{2,1,0:T(8,128)(2,1)S(1)} %bitcast.147), channel_id=1, replica_groups=mesh['wide'=8,'narrow'=4] {'wide'}, dimensions={0} | all-to-all | bytes 5242880 | tf_op jit(solution)/shard_map/all_to_all | solution.py:114
  292.4 67.7 %all-gather.2.cloned.1.call-done = bf16[40,128,8,128]{3,1,2,0:T(8,128)(2,1)} async-done(((bf16[40,32,8,128]{3,1,2,0:T(8,128)(2,1)}), bf16[40,128,8,128]{3,1,2,0:T(8,128)(2,1)}) %all-gather.2.cloned.1.call-update) | async-done | bytes 10485776 | tf_op jit(solution)/shard_map/all_gather | solution.py:121
  360.2 5.5 %convert_bitcast_fusion = bf16[40,32,8,128]{3,1,2,0:T(8,128)(2,1)S(1)} fusion(bf16[40,128,8,128]{3,1,2,0:T(8,128)(2,1)} %all-gather.2.cloned.1.call-done, bf16[128,128]{1,0:T(8,128)(2,1)} %param.27, s32[]{:T(128)S(6)} %select_n.28), kind=kOutput, calls=%fused_computation.27 | convolution fusion | flops 336855040 | bytes 13115396 | tf_op jit(solution)/shard_map/ab,dbrl->darl/dot_general | solution.py:118
  373.1 60.6 %while.21 = (s32[]{:T(128)}, f32[10,512,8]{1,2,0:T(8,128)S(1)}, s32[10,512]{1,0:T(8,128)S(1)}, bf16[1280,1024]{1,0:T(8,128)(2,1)S(1)}, bf16[10,512,128]{2,1,0:T(8,128)(2,1)}, /*index=5*/s32[]{:T(128)}) while((s32[]{:T(128)}, f32[10,512,8]{1,2,0:T(8,128)S(1)}, s32[10,512]{1,0:T(8,128)S(1)}, bf16[1280,1024]{1,0:T(8,128)(2,1)S(1)}, ...), condition=%wide.region_7.8_spmd, body=%wide.region_6.7_spmd.sunk | while | flops 1051138 | bytes 5730385 | solution.py:138
  434.5 5.4 reduce_sum.22
  440.9 5.5 %all-to-all-start.5 = ((f32[8,160,8]{1,2,0:T(8,128)}), f32[8,160,8]{1,2,0:T(8,128)S(1)}, u32[]{:S(2)}, u32[]{:S(2)}) async-start(f32[8,160,8]{1,2,0:T(8,128)} %copy.153), calls=%async_computation.5 | async-start | bytes 131072 | tf_op jit(solution)/shard_map/all_to_all | solution.py:144
  447.1 6.2 %all-to-all-done.5 = f32[8,160,8]{1,2,0:T(8,128)S(1)} async-done(((f32[8,160,8]{1,2,0:T(8,128)}), f32[8,160,8]{1,2,0:T(8,128)S(1)}, u32[]{:S(2)}, u32[]{:S(2)}) %all-to-all-start.5) | async-done | bytes 40992 | tf_op jit(solution)/shard_map/all_to_all | solution.py:144
  454.9 37.9 %all-reduce.3 = (f32[8,8]{0,1:T(8,128)S(1)}, f32[8,8]{1,0:T(8,128)S(1)}) all-reduce(f32[8,8]{0,1:T(8,128)S(1)} %copy-done.8, f32[8,8]{1,0:T(8,128)S(1)} %convolution_bitcast_fusion), channel_id=1, replica_groups=mesh['wide'=8,'narrow'=4] {'wide','narrow'}, use_global_device_ids=true, to_apply=%region_12.14 | all-reduce | flops 128 | bytes 1024 | tf_op jit(solution)/shard_map/psum | solution.py:149
  499.1 40.3 %psum.23 = f32[8,8]{1,0:T(8,128)S(1)} all-reduce(f32[8,8]{1,0:T(8,128)S(1)} %fusion.36), channel_id=1, replica_groups=mesh['wide'=8,'narrow'=4] {'wide','narrow'}, use_global_device_ids=true, to_apply=%region_13.17 | all-reduce | flops 64 | bytes 512 | tf_op jit(solution)/shard_map/psum | solution.py:155
  (212 shorter events, 136.4 us)
Async XLA Ops:
  7.2 211.1 %copy-start = (bf16[320,320]{1,0:T(8,128)(2,1)S(1)}, bf16[320,320]{1,0:T(8,128)(2,1)}, u32[]{:S(2)}) copy-start(bf16[320,320]{1,0:T(8,128)(2,1)} %param.26) | copy-start | bytes 614404
  10.8 0.6 copy-start.11
  14.7 10.6 %copy-start.3 = (f32[8,512]{1,0:T(8,128)S(1)}, f32[8,512]{1,0:T(8,128)}, u32[]{:S(2)}) copy-start(f32[8,512]{1,0:T(8,128)} %param.21) | copy-start | bytes 49156
  17.1 18.3 %copy-start.4 = (bf16[512,4,128]{2,1,0:T(4,128)(2,1)S(1)}, bf16[512,4,128]{2,1,0:T(4,128)(2,1)}, u32[]{:S(2)}) copy-start(bf16[512,4,128]{2,1,0:T(4,128)(2,1)} %param.23) | copy-start | bytes 1572868
  18.0 14.0 %all-to-all-start = ((s32[8,160,4]{1,2,0:T(4,128)}), s32[8,160,4]{1,2,0:T(4,128)S(1)}, u32[]{:S(2)}, u32[]{:S(2)}) async-start(s32[8,160,4]{1,2,0:T(4,128)} %copy.140), calls=%async_computation | async-start | bytes 65536 | tf_op jit(solution)/shard_map/all_to_all | solution.py:81
  32.0 10.0 %all-to-all-start.1 = ((bf16[8,160,8]{1,2,0:T(8,128)(2,1)}), bf16[8,160,8]{1,2,0:T(8,128)(2,1)S(1)}, u32[]{:S(2)}, u32[]{:S(2)}) async-start(bf16[8,160,8]{1,2,0:T(8,128)(2,1)} %copy.143), calls=%async_computation.1 | async-start | bytes 65536 | tf_op jit(solution)/shard_map/all_to_all | solution.py:74
  42.0 34.5 %all-to-all-start.2 = ((bf16[8,160,512]{2,1,0:T(8,128)(2,1)}), bf16[8,160,512]{2,1,0:T(8,128)(2,1)S(1)}, u32[]{:S(2)}, u32[]{:S(2)}) async-start(bf16[8,160,512]{2,1,0:T(8,128)(2,1)} %bitcast.17), calls=%async_computation.2 | async-start | bytes 2621440 | tf_op jit(solution)/shard_map/all_to_all | solution.py:67
  46.1 314.0 %all-gather.2.cloned.1.call-start = ((), (), s32[]{:S(2)}) async-start(), calls=%async_computation.6 | async-start | bytes 13107200 | tf_op jit(solution)/shard_map/all_gather | solution.py:121
  145.4 1.1 copy-start.2
  291.0 0.7 copy-start.6
  365.6 1.3 copy-start.7
  434.5 106.9 %copy-start.1 = (bf16[320,320]{1,0:T(8,128)(2,1)S(1)}, bf16[320,320]{1,0:T(8,128)(2,1)}, u32[]{:S(2)}) copy-start(bf16[320,320]{1,0:T(8,128)(2,1)} %param.26) | copy-start | bytes 614404
  440.0 14.8 %copy-start.10 = (f32[512]{0:T(512)S(1)}, f32[512]{0:T(512)}, u32[]{:S(2)}) copy-start(f32[512]{0:T(512)} %param.22) | copy-start | bytes 6148
  440.0 14.9 %copy-start.8 = (f32[8,8]{0,1:T(8,128)S(1)}, f32[8,8]{0,1:T(8,128)}, u32[]{:S(2)}) copy-start(f32[8,8]{0,1:T(8,128)} %fusion.35) | copy-start | bytes 772
  440.0 100.6 %copy-start.9 = (f32[8,512]{1,0:T(8,128)S(1)}, f32[8,512]{1,0:T(8,128)}, u32[]{:S(2)}) copy-start(f32[8,512]{1,0:T(8,128)} %param.19) | copy-start | bytes 49156
  440.9 12.4 %all-to-all-start.5 = ((f32[8,160,8]{1,2,0:T(8,128)}), f32[8,160,8]{1,2,0:T(8,128)S(1)}, u32[]{:S(2)}, u32[]{:S(2)}) async-start(f32[8,160,8]{1,2,0:T(8,128)} %copy.153), calls=%async_computation.5 | async-start | bytes 131072 | tf_op jit(solution)/shard_map/all_to_all | solution.py:144
  499.0 42.4 %copy-start.5 = (f32[8,512]{1,0:T(8,128)}, f32[8,512]{1,0:T(8,128)S(1)}, u32[]{:S(2)}) copy-start(f32[8,512]{1,0:T(8,128)S(1)} %convolution_subtract_fusion) | copy-start | bytes 49156
Sparse Core Ops, SparseCore 0:
  291.1 68.9 all-gather.1
where the time goes:
time: 550 us; the launch traced here: 548 us
  blocking collectives  204 us (37%)
  waiting for transfers between devices  107 us (19%)
  local copies, waits for them, and re-layouts  95.5 us (17%)
  matrix products  82 us (15%)
  other arithmetic  24.4 us (4%)
  starting transfers between devices  20.4 us (4%)
  between operations  14.4 us (3%)
    all_gather x1, waiting for transfers between devices, on_device(): lax.all_gather(timed_flux, 'narrow', axis=1, tiled=True)  67.7 us
    all_to_all x1, blocking collectives, on_device(): lax.all_to_all(flat_flux, 'wide', split_axis=1, concat_axis=0, tiled=True)  62.8 us
    all_to_all x1, blocking collectives, on_device(): lax.all_to_all(mixed_days, 'wide', split_axis=0, concat_axis=1, tiled=True)  62.7 us
    dot_general x10, matrix products, adjoint_step(): jnp.dot(weighted, foot_block, preferred_element_type=jnp.float32)  62.1 us
    psum x1, blocking collectives, on_device(): lax.psum(gram_matrix(residual_new, residual_new), ('wide', 'narrow'))  40.3 us
    psum x1, blocking collectives, on_device(): lax.psum((gram_matrix(direction, model_image), gram_matrix(residual, resi...  37.9 us
    all_to_all x1, waiting for transfers between devices, on_device(): lax.all_to_all(foot_rows[source].reshape(n_wide, capacity, tile_count * l...  28.6 us
    gather x10, local copies, waits for them, and re-layouts, forward_step(): picked = flux_table[id_block].reshape(rows_block, rhs_count, lon_count)  27.9 us
  transfers between devices with their start and end apart: 5, of which 5 were waited for; matrix products, arithmetic and copies ran while one was open for 2% of the time, Pallas kernels for 0%

commit v1 on v0

--- a/solution.py
+++ b/solution.py
@@ -5,6 +5,28 @@
 from jax.sharding import PartitionSpec as P
 
 HIGHEST = lax.Precision.HIGHEST
+
+
+def laid_out(pieces, dim):
+    pieces = jnp.moveaxis(pieces, 0, dim)
+    dims = pieces.shape
+    return pieces.reshape(*dims[:dim], dims[dim] * dims[dim + 1], *dims[dim + 2 :])
+
+
+def ring_gather(array, axis, dim):
+    size = lax.axis_size(axis)
+    pairs = [(i, (i + 1) % size) for i in range(size)]
+    back = [(b, a) for a, b in pairs]
+    lower, upper = ([], [])
+    for step in range(size - 1):
+        if step % 2 == 0:
+            lower.append(lax.ppermute(lower[-1] if lower else array, axis, pairs))
+        else:
+            upper.append(lax.ppermute(upper[-1] if upper else array, axis, back))
+    pieces = jnp.stack([*lower[::-1], array, *upper])
+    shift = lax.axis_index(axis) - len(lower)
+    pieces = pieces[(jnp.arange(size) - shift) % size]
+    return laid_out(pieces, dim)
 
 
 def chol_solve(matrix, right):
@@ -118,7 +140,7 @@
     lat_sum = jnp.einsum(
         "ab,dbrl->darl",
         lat_rows,
-        lax.all_gather(timed_flux, "narrow", axis=1, tiled=True),
+        ring_gather(timed_flux, "narrow", 1),
         preferred_element_type=jnp.float32,
     )
     spread_lat = lat_sum.astype(jnp.bfloat16)

time: 550 us -> 583 us (1.060)
  local copies, waits for them, and re-layouts: 95.5 us -> 115 us
  waiting for transfers between devices: 107 us -> 123 us
  between operations: 14.4 us -> 0.99 us
  other arithmetic: 24.4 us -> 34.3 us
    ppermute x0 -> x3, waiting for transfers between devices: none -> 83.1 us  [the longest x2 83.1 us: ring_gather(): lower.append(lax.ppermute(lower[-1] if lower else array, axis, pairs))]
    all_gather x1 -> x0, waiting for transfers between devices: 67.7 us -> none  [on_device(): lax.all_gather(timed_flux, 'narrow', axis=1, tiled=True)]
    gather x0 -> x8, local copies, waits for them, and re-layouts: none -> 20.9 us
    another operation x2 -> x3, other arithmetic: 1.16 us -> 11 us  [the longest x1 9.87 us: ring_gather(): pieces = jnp.stack([*lower[::-1], array, *upper])]
  transfers between devices with their start and end apart: 5 -> 7, of which waited for: 5 -> 6; matrix products, arithmetic and copies ran while one was open for 2% -> 3% of each run, Pallas kernels for 0% -> 0%
where the time goes in v1:
time: 583 us; the launch traced here: 582 us
  blocking collectives  206 us (35%)
  waiting for transfers between devices  123 us (21%)
  local copies, waits for them, and re-layouts  115 us (20%)
  matrix products  82.1 us (14%)
  other arithmetic  34.3 us (6%)
  starting transfers between devices  20.4 us (3%)
    ppermute x2, waiting for transfers between devices, ring_gather(): lower.append(lax.ppermute(lower[-1] if lower else array, axis, pairs))  83.1 us
    all_to_all x1, blocking collectives, on_device(): lax.all_to_all(flat_flux, 'wide', split_axis=1, concat_axis=0, tiled=True)  62.7 us
    all_to_all x1, blocking collectives, on_device(): lax.all_to_all(mixed_days, 'wide', split_axis=0, concat_axis=1, tiled=True)  62.7 us
    dot_general x10, matrix products, adjoint_step(): jnp.dot(weighted, foot_block, preferred_element_type=jnp.float32)  62.1 us
    psum x1, blocking collectives, on_device(): lax.psum(gram_matrix(residual_new, residual_new), ('wide', 'narrow'))  40.9 us
    psum x1, blocking collectives, on_device(): lax.psum((gram_matrix(direction, model_image), gram_matrix(residual, resi...  39.5 us
    all_to_all x1, waiting for transfers between devices, on_device(): lax.all_to_all(foot_rows[source].reshape(n_wide, capacity, tile_count * l...  28.7 us
    gather x10, local copies, waits for them, and re-layouts, forward_step(): picked = flux_table[id_block].reshape(rows_block, rhs_count, lon_count)  27.9 us
  transfers between devices with their start and end apart: 7, of which 6 were waited for; matrix products, arithmetic and copies ran while one was open for 3% of the time, Pallas kernels for 0%

profile of v1, /device:TPU:0, one launch (start us, length us, event | category | flops | bytes accessed | tf_op | source)
XLA Modules:
  0.0 581.7 jit_solution(3752493678111787520)
XLA Ops:
  11.5 7.3 %all-to-all-start = ((s32[8,160,4]{1,2,0:T(4,128)}), s32[8,160,4]{1,2,0:T(4,128)S(1)}, u32[]{:S(2)}, u32[]{:S(2)}) async-start(s32[8,160,4]{1,2,0:T(4,128)} %copy.152), calls=%async_computation | async-start | bytes 65536 | tf_op jit(solution)/shard_map/all_to_all | solution.py:103
  41.3 28.7 %all-to-all-done.2 = bf16[8,160,512]{2,1,0:T(8,128)(2,1)S(1)} async-done(((bf16[8,160,512]{2,1,0:T(8,128)(2,1)}), bf16[8,160,512]{2,1,0:T(8,128)(2,1)S(1)}, u32[]{:S(2)}, u32[]{:S(2)}) %all-to-all-start.2) | async-done | bytes 1310752 | tf_op jit(solution)/shard_map/all_to_all | solution.py:89
  70.8 68.1 %while.24 = (s32[]{:T(128)}, f32[10240,128]{1,0:T(8,128)}, s32[10,512]{1,0:T(8,128)S(1)}, bf16[10,512,8]{1,2,0:T(8,128)(2,1)S(1)}, bf16[10,512,128]{2,1,0:T(8,128)(2,1)S(1)}, /*index=5*/s32[]{:T(128)}, s32[]{:T(128)}) while((s32[]{:T(128)}, f32[10240,128]{1,0:T(8,128)}, s32[10,512]{1,0:T(8,128)S(1)}, ...), condition=%wide.region_5.6_spmd.clone, body=%wide.region_4.5_spmd.clone.sunk | while | flops 1351352320 | bytes 13269091 | solution.py:130
  76.7 6.4 %convolution_add_fusion.4 = f32[10240,128]{1,0:T(8,128)} fusion(f32[10240,128]{1,0:T(8,128)} %get-tuple-element.250, bf16[8,512]{1,0:T(8,128)(2,1)S(1)} %dynamic-slice_bitcast_fusion.5, bf16[1280,512]{1,0:T(8,128)(2,1)S(1)} %fusion.72, pred[]{:T(512)S(6)} %compare.39, bf16[10,512,128]{2,1,0:T(8,128)(2,1)S(1)} %get-tuple-element.260, ...), kind=kOutput, calls=%fused_computation.15.clone.1 | convolution fusion | flops 1350041600 | bytes 11935749 | tf_op jit(solution)/shard_map/while/body/eval_jaxpr/dot_general | solution.py:127
  83.6 6.4 %convolution_add_fusion.4 = f32[10240,128]{1,0:T(8,128)} fusion(f32[10240,128]{1,0:T(8,128)} %get-tuple-element.250, bf16[8,512]{1,0:T(8,128)(2,1)S(1)} %dynamic-slice_bitcast_fusion.5, bf16[1280,512]{1,0:T(8,128)(2,1)S(1)} %fusion.72, pred[]{:T(512)S(6)} %compare.39, bf16[10,512,128]{2,1,0:T(8,128)(2,1)S(1)} %get-tuple-element.260, ...), kind=kOutput, calls=%fused_computation.15.clone.1 | convolution fusion | flops 1350041600 | bytes 11935749 | tf_op jit(solution)/shard_map/while/body/eval_jaxpr/dot_general | solution.py:127
  90.6 6.4 %convolution_add_fusion.4 = f32[10240,128]{1,0:T(8,128)} fusion(f32[10240,128]{1,0:T(8,128)} %get-tuple-element.250, bf16[8,512]{1,0:T(8,128)(2,1)S(1)} %dynamic-slice_bitcast_fusion.5, bf16[1280,512]{1,0:T(8,128)(2,1)S(1)} %fusion.72, pred[]{:T(512)S(6)} %compare.39, bf16[10,512,128]{2,1,0:T(8,128)(2,1)S(1)} %get-tuple-element.260, ...), kind=kOutput, calls=%fused_computation.15.clone.1 | convolution fusion | flops 1350041600 | bytes 11935749 | tf_op jit(solution)/shard_map/while/body/eval_jaxpr/dot_general | solution.py:127
  97.6 6.4 %convolution_add_fusion.4 = f32[10240,128]{1,0:T(8,128)} fusion(f32[10240,128]{1,0:T(8,128)} %get-tuple-element.250, bf16[8,512]{1,0:T(8,128)(2,1)S(1)} %dynamic-slice_bitcast_fusion.5, bf16[1280,512]{1,0:T(8,128)(2,1)S(1)} %fusion.72, pred[]{:T(512)S(6)} %compare.39, bf16[10,512,128]{2,1,0:T(8,128)(2,1)S(1)} %get-tuple-element.260, ...), kind=kOutput, calls=%fused_computation.15.clone.1 | convolution fusion | flops 1350041600 | bytes 11935749 | tf_op jit(solution)/shard_map/while/body/eval_jaxpr/dot_general | solution.py:127
  104.6 6.4 %convolution_add_fusion.4 = f32[10240,128]{1,0:T(8,128)} fusion(f32[10240,128]{1,0:T(8,128)} %get-tuple-element.250, bf16[8,512]{1,0:T(8,128)(2,1)S(1)} %dynamic-slice_bitcast_fusion.5, bf16[1280,512]{1,0:T(8,128)(2,1)S(1)} %fusion.72, pred[]{:T(512)S(6)} %compare.39, bf16[10,512,128]{2,1,0:T(8,128)(2,1)S(1)} %get-tuple-element.260, ...), kind=kOutput, calls=%fused_computation.15.clone.1 | convolution fusion | flops 1350041600 | bytes 11935749 | tf_op jit(solution)/shard_map/while/body/eval_jaxpr/dot_general | solution.py:127
  111.6 6.4 %convolution_add_fusion.4 = f32[10240,128]{1,0:T(8,128)} fusion(f32[10240,128]{1,0:T(8,128)} %get-tuple-element.250, bf16[8,512]{1,0:T(8,128)(2,1)S(1)} %dynamic-slice_bitcast_fusion.5, bf16[1280,512]{1,0:T(8,128)(2,1)S(1)} %fusion.72, pred[]{:T(512)S(6)} %compare.39, bf16[10,512,128]{2,1,0:T(8,128)(2,1)S(1)} %get-tuple-element.260, ...), kind=kOutput, calls=%fused_computation.15.clone.1 | convolution fusion | flops 1350041600 | bytes 11935749 | tf_op jit(solution)/shard_map/while/body/eval_jaxpr/dot_general | solution.py:127
  118.5 6.4 %convolution_add_fusion.4 = f32[10240,128]{1,0:T(8,128)} fusion(f32[10240,128]{1,0:T(8,128)} %get-tuple-element.250, bf16[8,512]{1,0:T(8,128)(2,1)S(1)} %dynamic-slice_bitcast_fusion.5, bf16[1280,512]{1,0:T(8,128)(2,1)S(1)} %fusion.72, pred[]{:T(512)S(6)} %compare.39, bf16[10,512,128]{2,1,0:T(8,128)(2,1)S(1)} %get-tuple-element.260, ...), kind=kOutput, calls=%fused_computation.15.clone.1 | convolution fusion | flops 1350041600 | bytes 11935749 | tf_op jit(solution)/shard_map/while/body/eval_jaxpr/dot_general | solution.py:127
  125.5 6.4 %convolution_add_fusion.4 = f32[10240,128]{1,0:T(8,128)} fusion(f32[10240,128]{1,0:T(8,128)} %get-tuple-element.250, bf16[8,512]{1,0:T(8,128)(2,1)S(1)} %dynamic-slice_bitcast_fusion.5, bf16[1280,512]{1,0:T(8,128)(2,1)S(1)} %fusion.72, pred[]{:T(512)S(6)} %compare.39, bf16[10,512,128]{2,1,0:T(8,128)(2,1)S(1)} %get-tuple-element.260, ...), kind=kOutput, calls=%fused_computation.15.clone.1 | convolution fusion | flops 1350041600 | bytes 11935749 | tf_op jit(solution)/shard_map/while/body/eval_jaxpr/dot_general | solution.py:127
  132.5 6.4 %convolution_add_fusion.4 = f32[10240,128]{1,0:T(8,128)} fusion(f32[10240,128]{1,0:T(8,128)} %get-tuple-element.250, bf16[8,512]{1,0:T(8,128)(2,1)S(1)} %dynamic-slice_bitcast_fusion.5, bf16[1280,512]{1,0:T(8,128)(2,1)S(1)} %fusion.72, pred[]{:T(512)S(6)} %compare.39, bf16[10,512,128]{2,1,0:T(8,128)(2,1)S(1)} %get-tuple-element.260, ...), kind=kOutput, calls=%fused_computation.15.clone.1 | convolution fusion | flops 1350041600 | bytes 11935749 | tf_op jit(solution)/shard_map/while/body/eval_jaxpr/dot_general | solution.py:127
  149.0 62.7 %all_to_all.55 = bf16[40,8,4096]{2,0,1:T(8,128)(2,1)S(1)} all-to-all(bf16[40,8,4096]{2,0,1:T(8,128)(2,1)S(1)} %copy.159), channel_id=1, replica_groups=mesh['wide'=8,'narrow'=4] {'wide'}, dimensions={1} | all-to-all | bytes 5242880 | tf_op jit(solution)/shard_map/all_to_all | solution.py:132
  213.3 62.7 %all_to_all.56 = bf16[8,40,4096]{2,1,0:T(8,128)(2,1)S(1)} all-to-all(bf16[8,40,4096]{2,1,0:T(8,128)(2,1)S(1)} %bitcast.159), channel_id=1, replica_groups=mesh['wide'=8,'narrow'=4] {'wide'}, dimensions={0} | all-to-all | bytes 5242880 | tf_op jit(solution)/shard_map/all_to_all | solution.py:136
  282.3 55.9 %collective-permute-done = bf16[40,32,8,128]{3,2,1,0:T(8,128)(2,1)} collective-permute-done((bf16[40,32,8,128]{3,2,1,0:T(8,128)(2,1)}, bf16[40,32,8,128]{3,2,1,0:T(8,128)(2,1)}, u32[]{:S(2)}, u32[]{:S(2)}) %collective-permute-start) | collective-permute-done | bytes 2621472 | tf_op jit(solution)/shard_map/ppermute | solution.py:23
  342.4 27.2 %collective-permute-done.1 = bf16[40,32,8,128]{3,2,1,0:T(8,128)(2,1)} collective-permute-done((bf16[40,32,8,128]{3,2,1,0:T(8,128)(2,1)}, bf16[40,32,8,128]{3,2,1,0:T(8,128)(2,1)}, u32[]{:S(2)}, u32[]{:S(2)}) %collective-permute-start.1) | collective-permute-done | bytes 2621472 | tf_op jit(solution)/shard_map/ppermute | solution.py:23
  369.6 9.9 %pad_maximum_fusion = bf16[4,40,32,8,128]{4,3,2,1,0:T(8,128)(2,1)} fusion(bf16[1,40,32,8,128]{4,3,2,1,0:T(8,128)(2,1)} %bitcast.25, bf16[1,40,32,8,128]{4,3,2,1,0:T(8,128)(2,1)} %stack_reshape.3, bf16[1,40,32,8,128]{4,3,2,1,0:T(8,128)(2,1)} %bitcast.24, bf16[1,40,32,8,128]{4,3,2,1,0:T(8,128)(2,1)} %bitcast.23), kind=kLoop, calls=%fused_computation.28 | loop fusion | flops 15728640 | bytes 20971520 | tf_op jit(solution)/shard_map/stack | solution.py:26
  379.5 20.9 %while.23 = (s32[]{:T(128)}, bf16[4,40,32,8,128]{4,3,2,1,0:T(8,128)(2,1)}, s32[4,1]{0,1:T(1,128)S(1)}, bf16[4,40,32,8,128]{4,3,2,0,1:T(8,128)(2,1)}, s32[]{:T(128)}) while((s32[]{:T(128)}, bf16[4,40,32,8,128]{4,3,2,1,0:T(8,128)(2,1)}, s32[4,1]{0,1:T(1,128)S(1)}, bf16[4,40,32,8,128]{4,3,2,0,1:T(8,128)(2,1)}, s32[]{:T(128)}) %tuple.62), condition=%wide.while_cond, body=%wide.while_body.sunk | while | flops 2 | bytes 5243977 | solution.py:28
  400.4 5.5 convert_bitcast_fusion
  413.3 60.6 %while.22 = (s32[]{:T(128)}, f32[10,512,8]{1,2,0:T(8,128)S(1)}, s32[10,512]{1,0:T(8,128)S(1)}, bf16[1280,1024]{1,0:T(8,128)(2,1)S(1)}, bf16[10,512,128]{2,1,0:T(8,128)(2,1)}, /*index=5*/s32[]{:T(128)}) while((s32[]{:T(128)}, f32[10,512,8]{1,2,0:T(8,128)S(1)}, s32[10,512]{1,0:T(8,128)S(1)}, bf16[1280,1024]{1,0:T(8,128)(2,1)S(1)}, ...), condition=%wide.region_7.8_spmd, body=%wide.region_6.7_spmd.sunk | while | flops 1051138 | bytes 5730385 | solution.py:160
  474.7 5.4 reduce_sum.22
  485.4 6.2 %all-to-all-done.5 = f32[8,160,8]{1,2,0:T(8,128)S(1)} async-done(((f32[8,160,8]{1,2,0:T(8,128)}), f32[8,160,8]{1,2,0:T(8,128)S(1)}, u32[]{:S(2)}, u32[]{:S(2)}) %all-to-all-start.5) | async-done | bytes 40992 | tf_op jit(solution)/shard_map/all_to_all | solution.py:166
  493.1 39.5 %all-reduce.3 = (f32[8,8]{0,1:T(8,128)S(1)}, f32[8,8]{1,0:T(8,128)S(1)}) all-reduce(f32[8,8]{0,1:T(8,128)S(1)} %copy-done.8, f32[8,8]{1,0:T(8,128)S(1)} %convolution_bitcast_fusion), channel_id=1, replica_groups=mesh['wide'=8,'narrow'=4] {'wide','narrow'}, use_global_device_ids=true, to_apply=%region_12.14 | all-reduce | flops 128 | bytes 1024 | tf_op jit(solution)/shard_map/psum | solution.py:171
  538.9 40.9 %psum.23 = f32[8,8]{1,0:T(8,128)S(1)} all-reduce(f32[8,8]{1,0:T(8,128)S(1)} %fusion.41), channel_id=1, replica_groups=mesh['wide'=8,'narrow'=4] {'wide','narrow'}, use_global_device_ids=true, to_apply=%region_13.17 | all-reduce | flops 64 | bytes 512 | tf_op jit(solution)/shard_map/psum | solution.py:177
  (227 shorter events, 170.9 us)
Async XLA Ops:
  0.6 211.1 %copy-start = (bf16[320,320]{1,0:T(8,128)(2,1)S(1)}, bf16[320,320]{1,0:T(8,128)(2,1)}, u32[]{:S(2)}) copy-start(bf16[320,320]{1,0:T(8,128)(2,1)} %param.26) | copy-start | bytes 614404
  4.2 0.6 copy-start.11
  8.2 10.6 %copy-start.3 = (f32[8,512]{1,0:T(8,128)S(1)}, f32[8,512]{1,0:T(8,128)}, u32[]{:S(2)}) copy-start(f32[8,512]{1,0:T(8,128)} %param.21) | copy-start | bytes 49156
  10.5 18.3 %copy-start.4 = (bf16[512,4,128]{2,1,0:T(4,128)(2,1)S(1)}, bf16[512,4,128]{2,1,0:T(4,128)(2,1)}, u32[]{:S(2)}) copy-start(bf16[512,4,128]{2,1,0:T(4,128)(2,1)} %param.23) | copy-start | bytes 1572868
  11.5 14.0 %all-to-all-start = ((s32[8,160,4]{1,2,0:T(4,128)}), s32[8,160,4]{1,2,0:T(4,128)S(1)}, u32[]{:S(2)}, u32[]{:S(2)}) async-start(s32[8,160,4]{1,2,0:T(4,128)} %copy.152), calls=%async_computation | async-start | bytes 65536 | tf_op jit(solution)/shard_map/all_to_all | solution.py:103
  25.5 10.0 %all-to-all-start.1 = ((bf16[8,160,8]{1,2,0:T(8,128)(2,1)}), bf16[8,160,8]{1,2,0:T(8,128)(2,1)S(1)}, u32[]{:S(2)}, u32[]{:S(2)}) async-start(bf16[8,160,8]{1,2,0:T(8,128)(2,1)} %copy.155), calls=%async_computation.1 | async-start | bytes 65536 | tf_op jit(solution)/shard_map/all_to_all | solution.py:96
  35.4 34.5 %all-to-all-start.2 = ((bf16[8,160,512]{2,1,0:T(8,128)(2,1)}), bf16[8,160,512]{2,1,0:T(8,128)(2,1)S(1)}, u32[]{:S(2)}, u32[]{:S(2)}) async-start(bf16[8,160,512]{2,1,0:T(8,128)(2,1)} %bitcast.17), calls=%async_computation.2 | async-start | bytes 2621440 | tf_op jit(solution)/shard_map/all_to_all | solution.py:89
  138.9 1.1 copy-start.2
  277.4 61.1 %copy-start.6 = (f32[8,512]{1,0:T(8,128)S(1)}, f32[8,512]{1,0:T(8,128)}, u32[]{:S(2)}) copy-start(f32[8,512]{1,0:T(8,128)} %param.20) | copy-start | bytes 49156
  280.6 57.6 %collective-permute-start = (bf16[40,32,8,128]{3,2,1,0:T(8,128)(2,1)}, bf16[40,32,8,128]{3,2,1,0:T(8,128)(2,1)}, u32[]{:S(2)}, u32[]{:S(2)}) collective-permute-start(bf16[40,32,8,128]{3,2,1,0:T(8,128)(2,1)} %reshape.220), channel_id=1, source_target_pairs={{0,1},{1,2},{2,3},{3,0},{4,5},{5,6},{6,7},{7,4},{8,9},{9,10},{10,1... | collective-permute-start | bytes 7864328 | tf_op jit(solution)/shard_map/ppermute | solution.py:23
  280.6 61.8 %collective-permute-start.2 = (bf16[40,32,8,128]{3,2,1,0:T(8,128)(2,1)}, bf16[40,32,8,128]{3,2,1,0:T(8,128)(2,1)}, u32[]{:S(2)}, u32[]{:S(2)}) collective-permute-start(bf16[40,32,8,128]{3,2,1,0:T(8,128)(2,1)} %reshape.220), channel_id=1, source_target_pairs={{1,0},{2,1},{3,2},{0,3},{5,4},{6,5},{7,6},{4,7},{9,8},{10,9},{11,1... | collective-permute-start | bytes 7864328 | tf_op jit(solution)/shard_map/ppermute | solution.py:25
  338.2 31.4 %collective-permute-start.1 = (bf16[40,32,8,128]{3,2,1,0:T(8,128)(2,1)}, bf16[40,32,8,128]{3,2,1,0:T(8,128)(2,1)}, u32[]{:S(2)}, u32[]{:S(2)}) collective-permute-start(bf16[40,32,8,128]{3,2,1,0:T(8,128)(2,1)} %collective-permute-done), channel_id=1, source_target_pairs={{0,1},{1,2},{2,3},{3,0},{4,5},{5,6},{6,7},{7,4},{8,9},{9,10},{10,1... | collective-permute-start | bytes 7864328 | tf_op jit(solution)/shard_map/ppermute | solution.py:23
  405.9 1.3 copy-start.7
  474.7 107.0 %copy-start.1 = (bf16[320,320]{1,0:T(8,128)(2,1)S(1)}, bf16[320,320]{1,0:T(8,128)(2,1)}, u32[]{:S(2)}) copy-start(bf16[320,320]{1,0:T(8,128)(2,1)} %param.26) | copy-start | bytes 614404
  480.2 12.8 %copy-start.10 = (f32[512]{0:T(512)S(1)}, f32[512]{0:T(512)}, u32[]{:S(2)}) copy-start(f32[512]{0:T(512)} %param.22) | copy-start | bytes 6148
  480.2 12.9 %copy-start.8 = (f32[8,8]{0,1:T(8,128)S(1)}, f32[8,8]{0,1:T(8,128)}, u32[]{:S(2)}) copy-start(f32[8,8]{0,1:T(8,128)} %fusion.40) | copy-start | bytes 772
  480.2 100.7 %copy-start.9 = (f32[8,512]{1,0:T(8,128)S(1)}, f32[8,512]{1,0:T(8,128)}, u32[]{:S(2)}) copy-start(f32[8,512]{1,0:T(8,128)} %param.19) | copy-start | bytes 49156
  481.1 10.4 %all-to-all-start.5 = ((f32[8,160,8]{1,2,0:T(8,128)}), f32[8,160,8]{1,2,0:T(8,128)S(1)}, u32[]{:S(2)}, u32[]{:S(2)}) async-start(f32[8,160,8]{1,2,0:T(8,128)} %copy.167), calls=%async_computation.5 | async-start | bytes 131072 | tf_op jit(solution)/shard_map/all_to_all | solution.py:166
  538.7 43.0 %copy-start.5 = (f32[8,512]{1,0:T(8,128)}, f32[8,512]{1,0:T(8,128)S(1)}, u32[]{:S(2)}) copy-start(f32[8,512]{1,0:T(8,128)S(1)} %convolution_subtract_fusion) | copy-start | bytes 49156
